TPU v7x, 32 devices: a whole 2x2x4 slice. The times are simulated.
32 devices in a mesh: head: 4 (over y, x), seq: 8 (over z, core).
Axes of the slice: x: 2, y: 2, z: 4, core: 2. Of those that a mesh axis runs over, the one named last changes fastest.
Arguments:
- queries: bfloat16 [4096, 8192], P('seq', 'head'), may hold values from -200 to 200
- keys: bfloat16 [4096, 8192], P('seq', 'head'), may hold values from -6 to 6
- values: bfloat16 [4096, 8192], P('seq', 'head'), may hold values from -6 to 6
- cotangent: bfloat16 [4096, 8192], P('seq', 'head'), may hold values from -6 to 6
- prefix_keys: bfloat16 [4096, 8192], P('seq', 'head'), may hold values from -1.5 to 1.5
- prefix_values: bfloat16 [4096, 8192], P('seq', 'head'), may hold values from -1.5 to 1.5
- gain: float32 [8192], P('head'), may hold values from 0.5 to 1.5
- lengths: int32 [8], P('seq'), may hold values from 64 to 512, as said below
Outputs:
- normed: bfloat16 [4096, 8192], P('seq', 'head')
- query_grad: bfloat16 [4096, 8192], P('seq', 'head')
- key_grad: bfloat16 [4096, 8192], P('seq', 'head')
- value_grad: bfloat16 [4096, 8192], P('seq', 'head')
- prefix_key_grad: bfloat16 [4096, 8192], P('seq', 'head')
- prefix_value_grad: bfloat16 [4096, 8192], P('seq', 'head')
Inputs may be any that keep to these rules, and one draw needn't show every extreme that they name: `lengths`: one length per response; some response has exactly 512 live slots and some exactly 64.
All inputs are finite; a program needn't handle non-finite values.
Results may differ from a plain program's by a relative error of at most 0.0058.
Values sent between devices are 32-bit elements; how exact they have to be, the bound alone decides.
A program may use at most 128 MiB of HBM per device.

v0:
```python
import functools

import jax
import jax.numpy as jnp
from jax import lax
from jax.experimental import pallas as pl
from jax.experimental.pallas import tpu as pltpu
from jax.sharding import PartitionSpec as P

HEAD_DIM = 128
BLOCK = 256
EPS = 1e-06
MESH = pl.DeviceIdType.MESH
F32 = jnp.float32
BF16 = jnp.bfloat16
LEAD = 2
SUB = 1
SKEW = 3


def mm(a, b, ca, cb):
    return lax.dot_general(a, b, (((ca,), (cb,)), ((), ())), preferred_element_type=F32)


def kernel(nh, ns, width, *refs):
    (q_hbm, k_hbm, v_hbm, dy_hbm, pk_hbm, pv_hbm, gain_hbm, len_ref) = refs[:8]
    stage = refs[8:12]
    pk, pv, tout = refs[12:15]
    (q, k, v, dy, do, o, sc, mask, kv, mb, gb, sq, inn, rinv, coef) = refs[15:30]
    st_out, st_in = refs[30:32]
    bufs = (refs[32:41], refs[41:50])
    in_sem, st_send, st_recv, send_sem, recv_sem, gain_ref = refs[50:56]

    rows, cols = q.shape
    heads = cols // HEAD_DIM
    nown = heads // 2
    nb = rows // BLOCK
    nz = ns // 2
    me_h = lax.axis_index("head")
    me_s = lax.axis_index("seq")
    z = me_s // 2
    core = me_s % 2
    own0 = core * nown
    oth0 = (1 - core) * nown
    partner = (me_h, z * 2 + 1 - core)
    right = (me_h, jnp.minimum(me_s + 2, ns - 1))
    left = (me_h, jnp.maximum(me_s - 2, 0))
    not_first = z > 0
    not_last = z < nz - 1

    def cs(h):
        return pl.ds(pl.multiple_of(h * HEAD_DIM, HEAD_DIM), HEAD_DIM)

    half = nown * HEAD_DIM

    def load_half(j, src, dst, first):
        c = pl.ds(pl.multiple_of(first * HEAD_DIM, HEAD_DIM), half)
        return pltpu.make_async_copy(src.at[:, c], dst.at[:, c], in_sem.at[j])

    loads = [
        load_half(0, pk_hbm, pk, oth0),
        load_half(1, pv_hbm, pv, oth0),
        load_half(2, pk_hbm, pk, own0),
        load_half(3, pv_hbm, pv, own0),
        pltpu.make_async_copy(q_hbm, q, in_sem.at[4]),
        pltpu.make_async_copy(k_hbm, k, in_sem.at[5]),
        pltpu.make_async_copy(v_hbm, v, in_sem.at[6]),
        pltpu.make_async_copy(dy_hbm, dy, in_sem.at[7]),
        pltpu.make_async_copy(gain_hbm, gain_ref, in_sem.at[8]),
    ]
    for c in loads:
        c.start()

    barrier = pltpu.get_barrier_semaphore()
    pl.semaphore_signal(barrier, inc=1, device_id=partner, device_id_type=MESH)

    @pl.when(not_first)
    def _():
        pl.semaphore_signal(barrier, inc=1, device_id=left, device_id_type=MESH)

    @pl.when(not_last)
    def _():
        pl.semaphore_signal(barrier, inc=1, device_id=right, device_id_type=MESH)

    for d in range(1, nh):
        pl.semaphore_signal(
            barrier, inc=1, device_id=((me_h + d) % nh, me_s), device_id_type=MESH
        )

    live = lax.broadcasted_iota(jnp.int32, (rows, HEAD_DIM), 0) < len_ref[0]
    mask[...] = jnp.where(live, 1.0, 0.0).astype(BF16)
    sq[...] = jnp.zeros_like(sq)
    inn[...] = jnp.zeros_like(inn)
    pl.semaphore_wait(
        barrier, nh + not_first.astype(jnp.int32) + not_last.astype(jnp.int32)
    )
    for c in loads[:2]:
        c.wait()

    def causal():
        r = lax.broadcasted_iota(jnp.int32, (BLOCK, BLOCK), 0)
        c = lax.broadcasted_iota(jnp.int32, (BLOCK, BLOCK), 1)
        return r >= c

    def exchange(ph, produce, compute, consume, ready):
        xo, xi, x, rin, rout, lin, lout, tot, tin = bufs[ph]
        pieces = nown * SUB

        def hop(kind, src, dst, i, dev):
            return pltpu.make_async_remote_copy(
                src_ref=src,
                dst_ref=dst,
                send_sem=send_sem.at[ph, kind, i],
                recv_sem=recv_sem.at[ph, kind, i],
                device_id=dev,
                device_id_type=MESH,
            )

        def to_partner(i):
            return hop(0, xo.at[i], xi.at[i], i, partner)

        def total_out(i):
            return hop(1, tot.at[i], tin.at[i], i, partner)

        def to_right(i):
            return hop(2, rout.at[i // SUB, i % SUB], rin.at[i // SUB, i % SUB], i, right)

        def to_left(i):
            return hop(3, lout.at[i // SUB, i % SUB], lin.at[i // SUB, i % SUB], i, left)

        def split(state):
            return state.reshape(SUB, HEAD_DIM // SUB, HEAD_DIM)

        def give(i):
            xo[i] = split(produce(oth0 + i))
            to_partner(i).start()

        def first(i, carry):
            give(i)
            return carry

        lax.fori_loop(0, LEAD, first, 0)
        ready(-1)
        far = jnp.maximum(z, nz - 1 - z)
        late = max((SKEW * (nz - 1) + SUB - 1) // SUB + 2, nown)
        slots = max(heads, nown + late)

        def step(t):
            i_r = t - SKEW * z

            @pl.when((i_r >= 0) & (i_r < pieces))
            def _():
                i, j = i_r // SUB, i_r % SUB

                @pl.when(not_first)
                def _():
                    to_right(i_r).wait_recv()
                    rout[i, j] = rin[i, j] + x[i, j]

                @pl.when(jnp.logical_not(not_first))
                def _():
                    rout[i, j] = x[i, j]

                @pl.when(not_last)
                def _():
                    to_right(i_r).start()

            i_l = t - SKEW * (nz - 1 - z)

            @pl.when((i_l >= 0) & (i_l < pieces))
            def _():
                i, j = i_l // SUB, i_l % SUB

                @pl.when(not_last)
                def _():
                    to_left(i_l).wait_recv()
                    lout[i, j] = lin[i, j] + x[i, j]

                @pl.when(jnp.logical_not(not_last))
                def _():
                    lout[i, j] = x[i, j]

                @pl.when(not_first)
                def _():
                    to_left(i_l).start()

        def slot(s, carry):
            @pl.when(s + LEAD < nown)
            def _():
                give(s + LEAD)

            @pl.when(s < nown)
            def _():
                mine = split(produce(own0 + s))
                to_partner(s).wait_recv()
                x[s] = mine + xi[s]

            ready(s)
            for j in range(SUB):
                step(s * SUB + j)
                if j == 0:

                    @pl.when(s < heads)
                    def _():
                        for c in range(nb):
                            compute((own0 + s) % heads, c)

            i_t = s - (SKEW * far + SUB - 1) // SUB

            @pl.when((i_t >= 0) & (i_t < nown))
            def _():
                @pl.when(not_last)
                def _():
                    tot[i_t] = rout[i_t] + lin[i_t]

                @pl.when(jnp.logical_not(not_last))
                def _():
                    tot[i_t] = rout[i_t]

                total_out(i_t).start()
                consume(own0 + i_t, tot[i_t].reshape(HEAD_DIM, HEAD_DIM))

            i_o = s - late

            @pl.when((i_o >= 0) & (i_o < nown))
            def _():
                total_out(i_o).wait_recv()
                consume(oth0 + i_o, tin[i_o].reshape(HEAD_DIM, HEAD_DIM))

            return carry

        lax.fori_loop(0, slots, slot, 0)

        def drain(i, carry):
            to_partner(i).wait_send()
            total_out(i).wait_send()
            return carry

        lax.fori_loop(0, nown, drain, 0)

        def drain_hop(i, carry):
            @pl.when(not_last)
            def _():
                to_right(i).wait_send()

            @pl.when(not_first)
            def _():
                to_left(i).wait_send()

            return carry

        lax.fori_loop(0, pieces, drain_hop, 0)

    def blk(ref, c, h):
        return ref[pl.ds(c * BLOCK, BLOCK), cs(h)]

    def prefix_part(h):
        return mm(pk[:, cs(h)], pv[:, cs(h)], 0, 0)

    def intra(h, c):
        r = pl.ds(c * BLOCK, BLOCK)
        m = mask[r, :]
        qc, kc, vc = blk(q, c, h) * m, blk(k, c, h) * m, blk(v, c, h) * m
        q[r, cs(h)] = qc
        k[r, cs(h)] = kc
        v[r, cs(h)] = vc
        a = jnp.where(causal(), mm(qc, kc, 1, 1), 0.0).astype(BF16)
        sc[h, c] = a
        o[r, cs(h)] = mm(a, vc, 1, 0)
        if c < nb - 1:
            add = mm(kc, vc, 0, 0)
            kv[h, c] = add if c == 0 else kv[h, c - 1] + add

    def loaded(s):
        if isinstance(s, int):
            for c in loads[2:4]:
                c.wait()
            return

        @pl.when(s == 0)
        def _():
            for c in loads[4:7]:
                c.wait()

        @pl.when(s == 1)
        def _():
            loads[7].wait()
            loads[8].wait()

    def use_state(h, state):
        g = gain_ref[:, cs(h)]
        for c in range(nb):
            st = (state if c == 0 else state + kv[h, c - 1]).astype(BF16)
            mb[h, c] = st
            r = pl.ds(c * BLOCK, BLOCK)
            oc = o[r, cs(h)] + mm(blk(q, c, h), st, 1, 0)
            o[r, cs(h)] = oc
            dm = blk(dy, c, h) * mask[r, :]
            dy[r, cs(h)] = dm
            sq[r, :] += oc * oc
            inn[r, :] += dm.astype(F32) * g * oc

    exchange(0, prefix_part, intra, use_state, loaded)

    row_sq = jnp.sum(sq[...].T, axis=0, keepdims=True)
    row_in = jnp.sum(inn[...].T, axis=0, keepdims=True)
    st_out[...] = jnp.concatenate(
        [jnp.broadcast_to(row_sq, (4, rows)), jnp.broadcast_to(row_in, (4, rows))], axis=0
    )
    copies = []
    for d in range(1, nh):
        copies.append(
            pltpu.make_async_remote_copy(
                src_ref=st_out,
                dst_ref=st_in.at[d - 1],
                send_sem=st_send.at[d - 1],
                recv_sem=st_recv.at[d - 1],
                device_id=((me_h + d) % nh, me_s),
                device_id_type=MESH,
            )
        )
        copies[-1].start()
    total = st_out[...]
    for d in range(1, nh):
        copies[d - 1].wait_recv()
        total = total + st_in[d - 1]
    inv = 1.0 / jnp.sqrt(total[0:1] / width + EPS)
    cf = total[4:5] * (inv * inv * inv) / width
    rinv[...] = jnp.broadcast_to(inv, (HEAD_DIM, rows)).T
    coef[...] = jnp.broadcast_to(cf, (HEAD_DIM, rows)).T

    def state_grad(h):
        g = gain_ref[:, cs(h)]
        run = None
        for c in reversed(range(nb)):
            r = pl.ds(c * BLOCK, BLOCK)
            oc = o[r, cs(h)]
            ri = rinv[r, :]
            stage[0][r, cs(h)] = (g * oc * ri).astype(BF16)
            d = (blk(dy, c, h).astype(F32) * g * ri - oc * coef[r, :]).astype(BF16)
            do[r, cs(h)] = d
            if c < nb - 1:
                gb[h, c] = run.astype(BF16)
            part = mm(blk(q, c, h), d, 0, 0)
            run = part if run is None else run + part
        return run

    def grads(h, c):
        r = pl.ds(c * BLOCK, BLOCK)
        qc, kc, vc, dc = blk(q, c, h), blk(k, c, h), blk(v, c, h), blk(do, c, h)
        a = sc[h, c]
        p = jnp.where(causal(), mm(dc, vc, 1, 1), 0.0).astype(BF16)
        stage[1][r, cs(h)] = (mm(dc, mb[h, c], 1, 1) + mm(p, kc, 1, 0)).astype(BF16)
        kg = mm(p, qc, 0, 0)
        vg = mm(a, dc, 0, 0)
        if c < nb - 1:
            g = gb[h, c]
            kg = kg + mm(vc, g, 1, 1)
            vg = vg + mm(kc, g, 1, 0)
        stage[2][r, cs(h)] = kg.astype(BF16)
        stage[3][r, cs(h)] = vg.astype(BF16)

    def keep_total(h, state):
        tout[h] = state

    exchange(1, state_grad, grads, keep_total, lambda s: None)
    for c in copies:
        c.wait_send()


def finish(*refs):
    ready = refs[:4]
    pk, pv, total = refs[4:7]
    outs = refs[7:13]
    pkg, pvg, sem = refs[13:16]
    heads = total.shape[0]
    for j in range(4):
        pltpu.make_async_copy(ready[j], outs[j], sem.at[j]).start()

    def head(h, carry):
        c = pl.ds(pl.multiple_of(h * HEAD_DIM, HEAD_DIM), HEAD_DIM)
        state = total[h]
        hi = state.astype(BF16)
        lo = (state - hi.astype(F32)).astype(BF16)
        vals, keys = pv[:, c], pk[:, c]
        vv = jnp.concatenate([vals, vals], axis=1)
        kk = jnp.concatenate([keys, keys], axis=1)
        pkg[:, c] = mm(vv, jnp.concatenate([hi, lo], axis=1), 1, 1).astype(BF16)
        pvg[:, c] = mm(kk, jnp.concatenate([hi, lo], axis=0), 1, 0).astype(BF16)
        pltpu.make_async_copy(pkg.at[:, c], outs[4].at[:, c], sem.at[4]).start()
        pltpu.make_async_copy(pvg.at[:, c], outs[5].at[:, c], sem.at[5]).start()
        return carry

    lax.fori_loop(0, heads, head, 0)
    for j in range(4):
        pltpu.make_async_copy(ready[j], outs[j], sem.at[j]).wait()
    pltpu.make_async_copy(pkg, outs[4], sem.at[4]).wait()
    pltpu.make_async_copy(pvg, outs[5], sem.at[5]).wait()


def body(nh, ns, queries, keys, values, cotangent, prefix_keys, prefix_values, gain, lengths):
    rows, cols = queries.shape
    heads = cols // HEAD_DIM
    nown = heads // 2
    nb = rows // BLOCK
    any_spec = pl.BlockSpec(memory_space=pl.ANY)
    big = pltpu.VMEM((rows, cols), BF16)
    row = pltpu.VMEM((rows, HEAD_DIM), F32)
    states = [pltpu.VMEM((nown, SUB, HEAD_DIM // SUB, HEAD_DIM), F32)] * 9
    scratch = (
        [big] * 5
        + [
            pltpu.VMEM((rows, cols), F32),
            pltpu.VMEM((heads, nb, BLOCK, BLOCK), BF16),
            pltpu.VMEM((rows, HEAD_DIM), BF16),
            pltpu.VMEM((heads, max(nb - 1, 1), HEAD_DIM, HEAD_DIM), F32),
            pltpu.VMEM((heads, nb, HEAD_DIM, HEAD_DIM), BF16),
            pltpu.VMEM((heads, max(nb - 1, 1), HEAD_DIM, HEAD_DIM), BF16),
            row,
            row,
            row,
            row,
        ]
        + [pltpu.VMEM((8, rows), F32), pltpu.VMEM((max(nh - 1, 1), 8, rows), F32)]
        + states
        + states
        + [
            pltpu.SemaphoreType.DMA((9,)),
            pltpu.SemaphoreType.DMA((max(nh - 1, 1),)),
            pltpu.SemaphoreType.DMA((max(nh - 1, 1),)),
            pltpu.SemaphoreType.DMA((2, 4, nown * SUB)),
            pltpu.SemaphoreType.DMA((2, 4, nown * SUB)),
            pltpu.VMEM((1, cols), F32),
        ]
    )
    fast = pl.BlockSpec(memory_space=pltpu.VMEM)
    tot = pltpu.VMEM((heads, HEAD_DIM, HEAD_DIM), F32)
    wide = [queries, keys, values, cotangent, prefix_keys, prefix_values]
    wide.append(gain.reshape(1, cols))
    wide = [pltpu.with_memory_space_constraint(x, pltpu.HBM) for x in wide]
    made = pl.pallas_call(
        functools.partial(kernel, nh, ns, float(cols * nh)),
        out_shape=[big] * 6 + [tot],
        in_specs=[any_spec] * 7 + [pl.BlockSpec(memory_space=pltpu.SMEM)],
        out_specs=[fast] * 7,
        scratch_shapes=scratch,
        compiler_params=pltpu.CompilerParams(
            collective_id=0, has_side_effects=True, vmem_limit_bytes=36 * 1024 * 1024
        ),
    )(*wide, lengths)
    made = [pltpu.with_memory_space_constraint(x, pltpu.VMEM) for x in made]
    out = pltpu.HBM((rows, cols), BF16)
    return tuple(
        pl.pallas_call(
            finish,
            out_shape=[out] * 6,
            in_specs=[fast] * 7,
            out_specs=[any_spec] * 6,
            scratch_shapes=[big, big, pltpu.SemaphoreType.DMA((6,))],
            compiler_params=pltpu.CompilerParams(vmem_limit_bytes=8 * 1024 * 1024),
        )(*made)
    )


def solution(mesh):
    nh, ns = mesh.shape["head"], mesh.shape["seq"]
    tok = P("seq", "head")
    return jax.shard_map(
        functools.partial(body, nh, ns),
        mesh=mesh,
        in_specs=(tok,) * 6 + (P("head"), P("seq")),
        out_specs=(tok,) * 6,
        check_vma=False,
    )
```

profile of v0, /device:TPU:0, one launch (start us, length us, event | category | flops | bytes accessed | tf_op | source)
XLA Modules:
  0.0 65.3 jit_solution(16640650381762302524)
XLA Ops:
  1.3 58.4 %shard_map.127 = (bf16[512,2048]{1,0:T(8,128)(2,1)S(1)}, bf16[512,2048]{1,0:T(8,128)(2,1)S(1)}, bf16[512,2048]{1,0:T(8,128)(2,1)S(1)}, bf16[512,2048]{1,0:T(8,12...) custom-call(bf16[512,2048]{1,0:T(8,128)(2,1)} %refs_0_.1, ...), custom_call_target="tpu_custom_call" | custom-call | tf_op jit(solution)/shard_map/pallas_call | solution.py:441
  59.7 5.6 %shard_map.128 = (bf16[512,2048]{1,0:T(8,128)(2,1)}, bf16[512,2048]{1,0:T(8,128)(2,1)}, bf16[512,2048]{1,0:T(8,128)(2,1)}, bf16[512,2048]{1,0:T(8,128)(2,1)}, bf...) custom-call(bf16[512,2048]{1,0:T(8,128)(2,1)S(1)} %get-tuple-element.13.refs_0_, ...), custom_call_target="tpu_custom_call" | custom-call | tf_op jit(solution)/shard_map/pallas_call | solution.py:454
where the time goes:
time: 65.5 us; the launch traced here: 65.3 us
  Pallas kernels  64.1 us (98%)
  between operations  1.29 us (2%)
    pallas_call x1, Pallas kernels, body(): pl.pallas_call(functools.partial(kernel, nh, ns, float(cols * nh)), out_s...  58.4 us
    pallas_call x1, Pallas kernels, body(): pl.pallas_call(finish, out_shape=[out] * 6, in_specs=[fast] * 7, out_spec...  5.62 us

commit v1 on v0

v1 whole, which is shorter than its diff:
```python
import functools

import jax
import jax.numpy as jnp
from jax import lax
from jax.experimental import pallas as pl
from jax.experimental.pallas import tpu as pltpu
from jax.sharding import PartitionSpec as P

HEAD_DIM = 128
BLOCK = 256
EPS = 1e-06
MESH = pl.DeviceIdType.MESH
F32 = jnp.float32
BF16 = jnp.bfloat16
UNIT = 2
SUB = 2
SKEW = 3
STAGES = 2
PLAN = {
    4: (
        ([0, 3, 6, 9], [9, 6, 3, 0], [11, 11, 11, 11], [0, 0, 0, 0]),
        ([0, 3, 6, 9], [9, 6, 3, 0], [11, 11, 11, 11], [0, 0, 0, 0]),
    )
}


def mm(a, b, ca, cb):
    return lax.dot_general(a, b, (((ca,), (cb,)), ((), ())), preferred_element_type=F32)


def timetable(nz, units, ph):
    pieces = units * SUB
    far = SKEW * (nz - 1)
    if nz in PLAN:
        right, left, other, work = PLAN[nz][ph]
    else:
        right = [SKEW * k for k in range(nz)]
        left = [SKEW * (nz - 1 - k) for k in range(nz)]
        other, work = [far + SUB] * nz, [0] * nz
    rows = []
    for k in range(nz):
        own = max(right[k], left[k], work[k] + STAGES - SUB)
        oth = max(other[k], own, work[k] + (units + 1) * STAGES - SUB)
        last = max(pieces + own, pieces + oth, work[k] + 2 * units * STAGES)
        rows.append((right[k], left[k], own, oth, work[k], last))
    return rows


def kernel(nh, ns, width, *refs):
    (q_hbm, k_hbm, v_hbm, dy_hbm, pk_hbm, pv_hbm, gain_hbm, len_ref) = refs[:8]
    stage = refs[8:12]
    pk, pv, tout = refs[12:15]
    (q, k, v, dy, do, o, sc, ps, kv, mb, gb, sq, inn, rinv, coef) = refs[15:30]
    st_out, st_in = refs[30:32]
    bufs = (refs[32:41], refs[41:50])
    in_sem, st_send, st_recv, send_sem, recv_sem, gain_ref = refs[50:56]

    rows, cols = q.shape
    heads = cols // HEAD_DIM
    nown = heads // 2
    units = nown // UNIT
    nb = rows // BLOCK
    nz = ns // 2
    me_h = lax.axis_index("head")
    me_s = lax.axis_index("seq")
    z = me_s // 2
    core = me_s % 2
    own0 = core * nown
    oth0 = (1 - core) * nown
    partner = (me_h, z * 2 + 1 - core)
    right = (me_h, jnp.minimum(me_s + 2, ns - 1))
    left = (me_h, jnp.maximum(me_s - 2, 0))
    not_first = z > 0
    not_last = z < nz - 1

    def cs(h):
        return pl.ds(pl.multiple_of(h * HEAD_DIM, HEAD_DIM), HEAD_DIM)

    def part(j, src, dst, head, count):
        c = pl.ds(pl.multiple_of(head * HEAD_DIM, HEAD_DIM), count * HEAD_DIM)
        return pltpu.make_async_copy(src.at[:, c], dst.at[:, c], in_sem.at[j])

    loads = [
        part(0, pk_hbm, pk, oth0, UNIT),
        part(1, pv_hbm, pv, oth0, UNIT),
        part(2, pk_hbm, pk, oth0 + UNIT, nown - UNIT),
        part(3, pv_hbm, pv, oth0 + UNIT, nown - UNIT),
        part(4, pk_hbm, pk, own0, nown),
        part(5, pv_hbm, pv, own0, nown),
        pltpu.make_async_copy(q_hbm, q, in_sem.at[6]),
        pltpu.make_async_copy(k_hbm, k, in_sem.at[7]),
        pltpu.make_async_copy(v_hbm, v, in_sem.at[8]),
        pltpu.make_async_copy(dy_hbm, dy, in_sem.at[9]),
        pltpu.make_async_copy(gain_hbm, gain_ref, in_sem.at[10]),
    ]
    for c in loads[:6]:
        c.start()

    barrier = pltpu.get_barrier_semaphore()
    pl.semaphore_signal(barrier, inc=1, device_id=partner, device_id_type=MESH)

    @pl.when(not_first)
    def _():
        pl.semaphore_signal(barrier, inc=1, device_id=left, device_id_type=MESH)

    @pl.when(not_last)
    def _():
        pl.semaphore_signal(barrier, inc=1, device_id=right, device_id_type=MESH)

    for d in range(1, nh):
        pl.semaphore_signal(
            barrier, inc=1, device_id=((me_h + d) % nh, me_s), device_id_type=MESH
        )

    sq[...] = jnp.zeros_like(sq)
    inn[...] = jnp.zeros_like(inn)
    for c in loads[:2]:
        c.wait()
    for c in loads[6:]:
        c.start()

    def causal():
        r = lax.broadcasted_iota(jnp.int32, (BLOCK, BLOCK), 0)
        c = lax.broadcasted_iota(jnp.int32, (BLOCK, BLOCK), 1)
        return r >= c

    def pick(values):
        found = jnp.int32(0)
        for k, value in enumerate(values):
            found = found + (z == k).astype(jnp.int32) * value
        return found

    plans = [timetable(nz, units, ph) for ph in range(2)]

    def exchange(ph, produce, compute, consume, ready):
        xo, xi, x, rin, rout, lin, lout, tot, tin = bufs[ph]
        pieces = units * SUB

        def hop(kind, src, dst, i, dev):
            return pltpu.make_async_remote_copy(
                src_ref=src,
                dst_ref=dst,
                send_sem=send_sem.at[ph, kind],
                recv_sem=recv_sem.at[ph, kind, i],
                device_id=dev,
                device_id_type=MESH,
            )

        def to_partner(u):
            return hop(0, xo.at[u], xi.at[u], u, partner)

        def total_out(i):
            return hop(1, tot.at[i // SUB, i % SUB], tin.at[i // SUB, i % SUB], i, partner)

        def to_right(i):
            return hop(2, rout.at[i // SUB, i % SUB], rin.at[i // SUB, i % SUB], i, right)

        def to_left(i):
            return hop(3, lout.at[i // SUB, i % SUB], lin.at[i // SUB, i % SUB], i, left)

        def make(dst, u, first):
            for j, state in enumerate(produce(first + u * UNIT)):
                per = SUB // UNIT
                dst[u, j * per : (j + 1) * per] = state.reshape(per, -1, HEAD_DIM)

        def give(u):
            make(xo, u, oth0)
            to_partner(u).start()

        def states(ref, u):
            per = SUB // UNIT
            return [
                ref[u, j * per : (j + 1) * per].reshape(HEAD_DIM, HEAD_DIM) for j in range(UNIT)
            ]

        make(xo, 0, oth0)
        ready(-2)
        to_partner(0).start()
        ready(-1)
        plan = [pick([p[j] for p in plans[ph]]) for j in range(6)]
        r_at, l_at, t_at, o_at, c_at, slots = plan

        def slot(s, carry):
            u = s // SUB
            fresh = s % SUB == 0

            @pl.when(fresh & (u + 1 < units))
            def _():
                give(u + 1)

            @pl.when(fresh & (u < units))
            def _():
                make(x, u, own0)
                to_partner(u).wait_recv()
                x[u] = x[u] + xi[u]

            i_r = s - r_at

            @pl.when((i_r >= 0) & (i_r < pieces))
            def _():
                i, j = i_r // SUB, i_r % SUB

                @pl.when(not_first)
                def _():
                    to_right(i_r).wait_recv()
                    rout[i, j] = rin[i, j] + x[i, j]

                @pl.when(jnp.logical_not(not_first))
                def _():
                    rout[i, j] = x[i, j]

                @pl.when(not_last)
                def _():
                    to_right(i_r).start()

            i_l = s - l_at

            @pl.when((i_l >= 0) & (i_l < pieces))
            def _():
                i, j = i_l // SUB, i_l % SUB

                @pl.when(not_last)
                def _():
                    to_left(i_l).wait_recv()
                    lout[i, j] = lin[i, j] + x[i, j]

                @pl.when(jnp.logical_not(not_last))
                def _():
                    lout[i, j] = x[i, j]

                @pl.when(not_first)
                def _():
                    to_left(i_l).start()

            i_t = s - t_at

            @pl.when((i_t >= 0) & (i_t < pieces))
            def _():
                i, j = i_t // SUB, i_t % SUB

                @pl.when(not_last)
                def _():
                    tot[i, j] = rout[i, j] + lin[i, j]

                @pl.when(jnp.logical_not(not_last))
                def _():
                    tot[i, j] = rout[i, j]

                total_out(i_t).start()

            work = s - c_at
            ready(work)

            @pl.when((work >= 0) & (work < 2 * units * STAGES))
            def _():
                h = (own0 + work // STAGES * UNIT) % heads
                for c in range(STAGES):

                    @pl.when(work % STAGES == c)
                    def _(c=c):
                        compute[c](h)

            @pl.when((i_t >= 0) & (i_t < pieces) & (i_t % SUB == SUB - 1))
            def _():
                i = i_t // SUB
                consume(own0 + i * UNIT, states(tot, i))

            i_o = s - o_at

            @pl.when((i_o >= 0) & (i_o < pieces) & (i_o % SUB == SUB - 1))
            def _():
                i = i_o // SUB
                for j in range(SUB):
                    total_out(i * SUB + j).wait_recv()
                consume(oth0 + i * UNIT, states(tin, i))

            return carry

        lax.fori_loop(0, slots, slot, 0)

        hop(0, xo, xi, 0, partner).wait_send()
        hop(1, tot, tin, 0, partner).wait_send()

        @pl.when(not_last)
        def _():
            hop(2, rout, rin, 0, right).wait_send()

        @pl.when(not_first)
        def _():
            hop(3, lout, lin, 0, left).wait_send()

    def blk(ref, c, h):
        return ref[pl.ds(c * BLOCK, BLOCK), cs(h)]

    def prefix_part(h):
        return [mm(pk[:, cs(h + j)], pv[:, cs(h + j)], 0, 0) for j in range(UNIT)]

    items = [(j, c) for j in range(UNIT) for c in range(nb)]

    def score(h):
        seen = causal()
        for j, c in items:
            a = mm(blk(q, c, h + j), blk(k, c, h + j), 1, 1)
            sc[h + j, c] = jnp.where(seen, a, 0.0).astype(BF16)

    def attend(h):
        for j, c in items:
            vc = blk(v, c, h + j)
            o[pl.ds(c * BLOCK, BLOCK), cs(h + j)] = mm(sc[h + j, c], vc, 1, 0)
            if c < nb - 1:
                add = mm(blk(k, c, h + j), vc, 0, 0)
                kv[h + j, c] = add if c == 0 else kv[h + j, c - 1] + add

    def loaded(s):
        if isinstance(s, int):
            if s == -2:
                pl.semaphore_wait(
                    barrier, nh + not_first.astype(jnp.int32) + not_last.astype(jnp.int32)
                )
            else:
                for c in loads[2:6]:
                    c.wait()
            return

        @pl.when(s == 0)
        def _():
            for c in loads[6:9]:
                c.wait()

        @pl.when(s == 1)
        def _():
            loads[9].wait()
            loads[10].wait()

    def use_state(h, got):
        for c in range(nb):
            r = pl.ds(c * BLOCK, BLOCK)
            squares, inner = sq[r, :], inn[r, :]
            for j, state in enumerate(got):
                st = (state if c == 0 else state + kv[h + j, c - 1]).astype(BF16)
                mb[h + j, c] = st
                oc = o[r, cs(h + j)] + mm(blk(q, c, h + j), st, 1, 0)
                o[r, cs(h + j)] = oc
                squares = squares + oc * oc
                inner = inner + blk(dy, c, h + j).astype(F32) * gain_ref[:, cs(h + j)] * oc
            sq[r, :] = squares
            inn[r, :] = inner

    exchange(0, prefix_part, (score, attend), use_state, loaded)

    row_sq = jnp.sum(sq[...].T, axis=0, keepdims=True)
    row_in = jnp.sum(inn[...].T, axis=0, keepdims=True)
    lanes = rows // HEAD_DIM

    def fold(row):
        return [row[:, i * HEAD_DIM : (i + 1) * HEAD_DIM] for i in range(lanes)]

    def unfold(tile, first):
        return jnp.concatenate([tile[first + i : first + i + 1] for i in range(lanes)], axis=1)

    st_out[...] = jnp.concatenate(fold(row_sq) + fold(row_in), axis=0)
    copies = []
    for d in range(1, nh):
        copies.append(
            pltpu.make_async_remote_copy(
                src_ref=st_out,
                dst_ref=st_in.at[d - 1],
                send_sem=st_send.at[d - 1],
                recv_sem=st_recv.at[d - 1],
                device_id=((me_h + d) % nh, me_s),
                device_id_type=MESH,
            )
        )
        copies[-1].start()
    total = st_out[...]
    for d in range(1, nh):
        copies[d - 1].wait_recv()
        total = total + st_in[d - 1]
    inv = 1.0 / jnp.sqrt(unfold(total, 0) / width + EPS)
    cf = unfold(total, lanes) * (inv * inv * inv) / width
    live = lax.broadcasted_iota(jnp.int32, (1, rows), 1) < len_ref[0]
    inv = jnp.where(live, inv, 0.0)
    cf = jnp.where(live, cf, 0.0)
    rinv[...] = jnp.broadcast_to(inv, (HEAD_DIM, rows)).T
    coef[...] = jnp.broadcast_to(cf, (HEAD_DIM, rows)).T

    def state_grad(h):
        run = [None] * UNIT
        for c in reversed(range(nb)):
            r = pl.ds(c * BLOCK, BLOCK)
            ri, cf = rinv[r, :], coef[r, :]
            for j in range(UNIT):
                g = gain_ref[:, cs(h + j)]
                oc = o[r, cs(h + j)]
                stage[0][r, cs(h + j)] = (g * oc * ri).astype(BF16)
                d = (blk(dy, c, h + j).astype(F32) * g * ri - oc * cf).astype(BF16)
                do[r, cs(h + j)] = d
                if c < nb - 1:
                    gb[h + j, c] = run[j].astype(BF16)
                part = mm(blk(q, c, h + j), d, 0, 0)
                run[j] = part if run[j] is None else run[j] + part
        return run

    def query_side(h):
        seen = causal()
        for j, c in items:
            dc = blk(do, c, h + j)
            p = jnp.where(seen, mm(dc, blk(v, c, h + j), 1, 1), 0.0).astype(BF16)
            ps[0, j, c] = p
            qg = mm(dc, mb[h + j, c], 1, 1) + mm(p, blk(k, c, h + j), 1, 0)
            stage[1][pl.ds(c * BLOCK, BLOCK), cs(h + j)] = qg.astype(BF16)

    def key_side(h):
        for j, c in items:
            r = pl.ds(c * BLOCK, BLOCK)
            kg = mm(ps[0, j, c], blk(q, c, h + j), 0, 0)
            vg = mm(sc[h + j, c], blk(do, c, h + j), 0, 0)
            if c < nb - 1:
                g = gb[h + j, c]
                kg = kg + mm(blk(v, c, h + j), g, 1, 1)
                vg = vg + mm(blk(k, c, h + j), g, 1, 0)
            stage[2][r, cs(h + j)] = kg.astype(BF16)
            stage[3][r, cs(h + j)] = vg.astype(BF16)

    def keep_total(h, got):
        for j, state in enumerate(got):
            tout[h + j] = state

    exchange(1, state_grad, (query_side, key_side), keep_total, lambda s: None)
    for c in copies:
        c.wait_send()


def finish(*refs):
    ready = refs[:4]
    pk, pv, total = refs[4:7]
    outs = refs[7:13]
    pkg, pvg, sem = refs[13:16]
    heads = total.shape[0]
    for j in range(4):
        pltpu.make_async_copy(ready[j], outs[j], sem.at[j]).start()

    def head(h, carry):
        c = pl.ds(pl.multiple_of(h * HEAD_DIM, HEAD_DIM), HEAD_DIM)
        state = total[h]
        hi = state.astype(BF16)
        lo = (state - hi.astype(F32)).astype(BF16)
        vals, keys = pv[:, c], pk[:, c]
        vv = jnp.concatenate([vals, vals], axis=1)
        kk = jnp.concatenate([keys, keys], axis=1)
        pkg[:, c] = mm(vv, jnp.concatenate([hi, lo], axis=1), 1, 1).astype(BF16)
        pvg[:, c] = mm(kk, jnp.concatenate([hi, lo], axis=0), 1, 0).astype(BF16)
        pltpu.make_async_copy(pkg.at[:, c], outs[4].at[:, c], sem.at[4]).start()
        pltpu.make_async_copy(pvg.at[:, c], outs[5].at[:, c], sem.at[5]).start()
        return carry

    lax.fori_loop(0, heads, head, 0)
    for j in range(4):
        pltpu.make_async_copy(ready[j], outs[j], sem.at[j]).wait()
    pltpu.make_async_copy(pkg, outs[4], sem.at[4]).wait()
    pltpu.make_async_copy(pvg, outs[5], sem.at[5]).wait()


def body(nh, ns, queries, keys, values, cotangent, prefix_keys, prefix_values, gain, lengths):
    rows, cols = queries.shape
    heads = cols // HEAD_DIM
    nown = heads // 2
    nb = rows // BLOCK
    any_spec = pl.BlockSpec(memory_space=pl.ANY)
    big = pltpu.VMEM((rows, cols), BF16)
    row = pltpu.VMEM((rows, HEAD_DIM), F32)
    units = nown // UNIT
    states = [pltpu.VMEM((units, SUB, UNIT * HEAD_DIM // SUB, HEAD_DIM), F32)] * 9
    scratch = (
        [big] * 5
        + [
            pltpu.VMEM((rows, cols), F32),
            pltpu.VMEM((heads, nb, BLOCK, BLOCK), BF16),
            pltpu.VMEM((1, UNIT, nb, BLOCK, BLOCK), BF16),
            pltpu.VMEM((heads, max(nb - 1, 1), HEAD_DIM, HEAD_DIM), F32),
            pltpu.VMEM((heads, nb, HEAD_DIM, HEAD_DIM), BF16),
            pltpu.VMEM((heads, max(nb - 1, 1), HEAD_DIM, HEAD_DIM), BF16),
            row,
            row,
            row,
            row,
        ]
        + [
            pltpu.VMEM((2 * rows // HEAD_DIM, HEAD_DIM), F32),
            pltpu.VMEM((max(nh - 1, 1), 2 * rows // HEAD_DIM, HEAD_DIM), F32),
        ]
        + states
        + states
        + [
            pltpu.SemaphoreType.DMA((11,)),
            pltpu.SemaphoreType.DMA((max(nh - 1, 1),)),
            pltpu.SemaphoreType.DMA((max(nh - 1, 1),)),
            pltpu.SemaphoreType.DMA((2, 4)),
            pltpu.SemaphoreType.DMA((2, 4, units * SUB)),
            pltpu.VMEM((1, cols), F32),
        ]
    )
    fast = pl.BlockSpec(memory_space=pltpu.VMEM)
    tot = pltpu.VMEM((heads, HEAD_DIM, HEAD_DIM), F32)
    wide = [queries, keys, values, cotangent, prefix_keys, prefix_values]
    wide.append(gain.reshape(1, cols))
    wide = [pltpu.with_memory_space_constraint(x, pltpu.HBM) for x in wide]
    made = pl.pallas_call(
        functools.partial(kernel, nh, ns, float(cols * nh)),
        out_shape=[big] * 6 + [tot],
        in_specs=[any_spec] * 7 + [pl.BlockSpec(memory_space=pltpu.SMEM)],
        out_specs=[fast] * 7,
        scratch_shapes=scratch,
        compiler_params=pltpu.CompilerParams(
            collective_id=0, has_side_effects=True, vmem_limit_bytes=38 * 1024 * 1024
        ),
    )(*wide, lengths)
    made = [pltpu.with_memory_space_constraint(x, pltpu.VMEM) for x in made]
    out = pltpu.HBM((rows, cols), BF16)
    return tuple(
        pl.pallas_call(
            finish,
            out_shape=[out] * 6,
            in_specs=[fast] * 7,
            out_specs=[any_spec] * 6,
            scratch_shapes=[big, big, pltpu.SemaphoreType.DMA((6,))],
            compiler_params=pltpu.CompilerParams(vmem_limit_bytes=8 * 1024 * 1024),
        )(*made)
    )


def solution(mesh):
    nh, ns = mesh.shape["head"], mesh.shape["seq"]
    tok = P("seq", "head")
    return jax.shard_map(
        functools.partial(body, nh, ns),
        mesh=mesh,
        in_specs=(tok,) * 6 + (P("head"), P("seq")),
        out_specs=(tok,) * 6,
        check_vma=False,
    )
```

time: 65.5 us -> 64 us (0.977)
  Pallas kernels: 64.1 us -> 62.6 us
    pallas_call x1, Pallas kernels: 58.4 us -> 57 us  [body(): pl.pallas_call(functools.partial(kernel, nh, ns, float(cols * nh)), out_s...]
where the time goes in v1:
time: 64 us; the launch traced here: 63.9 us
  Pallas kernels  62.6 us (98%)
  between operations  1.29 us (2%)
    pallas_call x1, Pallas kernels, body(): pl.pallas_call(functools.partial(kernel, nh, ns, float(cols * nh)), out_s...  57 us
    pallas_call x1, Pallas kernels, body(): pl.pallas_call(finish, out_shape=[out] * 6, in_specs=[fast] * 7, out_spec...  5.62 us

profile of v1, /device:TPU:0, one launch (start us, length us, event | category | flops | bytes accessed | tf_op | source)
XLA Modules:
  0.0 63.9 jit_solution(17868436755818591188)
XLA Ops:
  1.3 57.0 %shard_map.127 = (bf16[512,2048]{1,0:T(8,128)(2,1)S(1)}, bf16[512,2048]{1,0:T(8,128)(2,1)S(1)}, bf16[512,2048]{1,0:T(8,128)(2,1)S(1)}, bf16[512,2048]{1,0:T(8,12...) custom-call(bf16[512,2048]{1,0:T(8,128)(2,1)} %refs_0_.1, ...), custom_call_target="tpu_custom_call" | custom-call | tf_op jit(solution)/shard_map/pallas_call | solution.py:509
  58.2 5.6 %shard_map.128 = (bf16[512,2048]{1,0:T(8,128)(2,1)}, bf16[512,2048]{1,0:T(8,128)(2,1)}, bf16[512,2048]{1,0:T(8,128)(2,1)}, bf16[512,2048]{1,0:T(8,128)(2,1)}, bf...) custom-call(bf16[512,2048]{1,0:T(8,128)(2,1)S(1)} %get-tuple-element.13.refs_0_, ...), custom_call_target="tpu_custom_call" | custom-call | tf_op jit(solution)/shard_map/pallas_call | solution.py:522

commit v2 on v1

--- a/solution.py
+++ b/solution.py
@@ -17,10 +17,12 @@
 SUB = 2
 SKEW = 3
 STAGES = 2
+AHEAD = 2
+GROUP = 4
 PLAN = {
     4: (
-        ([0, 3, 6, 9], [9, 6, 3, 0], [11, 11, 11, 11], [0, 0, 0, 0]),
-        ([0, 3, 6, 9], [9, 6, 3, 0], [11, 11, 11, 11], [0, 0, 0, 0]),
+        ([0, 3, 6, 9], [9, 6, 3, 0], [10, 7, 7, 10], [(4, 2, 1, 16, 99, 1, 1), (2, 1, 1, 16, 99, 1, 1), (2, 1, 1, 16, 99, 1, 1), (4, 2, 1, 16, 99, 1, 1)]),
+        ([0, 3, 6, 9], [9, 6, 3, 0], [10, 7, 7, 10], [(4, 2, 1, 10, 9, 1, 1), (2, 1, 1, 16, 99, 1, 1), (2, 1, 1, 16, 99, 1, 1), (4, 2, 1, 10, 9, 1, 1)]),
     )
 }
 
@@ -29,21 +31,45 @@
     return lax.dot_general(a, b, (((ca,), (cb,)), ((), ())), preferred_element_type=F32)
 
 
+def clip(value, top):
+    if isinstance(value, int):
+        return min(max(value, 0), top)
+    return jnp.minimum(jnp.maximum(value, 0), top)
+
+
+def done_by(s, row, total):
+    first, up, down, count, second, up2, down2 = row
+    fast = clip((s + 1 - first) * up // down, count)
+    return fast + clip((s + 1 - second) * up2 // down2, total - count)
+
+
 def timetable(nz, units, ph):
     pieces = units * SUB
-    far = SKEW * (nz - 1)
+    total = 2 * units * STAGES
     if nz in PLAN:
         right, left, other, work = PLAN[nz][ph]
     else:
         right = [SKEW * k for k in range(nz)]
         left = [SKEW * (nz - 1 - k) for k in range(nz)]
-        other, work = [far + SUB] * nz, [0] * nz
+        other, work = [SKEW * (nz - 1) + SUB] * nz, [(2, 1, 1, total, 0, 1, 1)] * nz
     rows = []
     for k in range(nz):
-        own = max(right[k], left[k], work[k] + STAGES - SUB)
-        oth = max(other[k], own, work[k] + (units + 1) * STAGES - SUB)
-        last = max(pieces + own, pieces + oth, work[k] + 2 * units * STAGES)
-        rows.append((right[k], left[k], own, oth, work[k], last))
+        own = max(right[k], left[k])
+        while any(
+            done_by(u * SUB + own, work[k], total) < (u + 1) * STAGES
+            for u in range(units)
+        ):
+            own += 1
+        oth = max(other[k], own)
+        while any(
+            done_by(u * SUB + oth, work[k], total) < (units + u + 1) * STAGES
+            for u in range(units)
+        ):
+            oth += 1
+        last = pieces + oth
+        while done_by(last - 1, work[k], total) < total:
+            last += 1
+        rows.append((right[k], left[k], own, oth, last) + tuple(work[k]))
     return rows
 
 
@@ -84,17 +110,19 @@
     loads = [
         part(0, pk_hbm, pk, oth0, UNIT),
         part(1, pv_hbm, pv, oth0, UNIT),
-        part(2, pk_hbm, pk, oth0 + UNIT, nown - UNIT),
-        part(3, pv_hbm, pv, oth0 + UNIT, nown - UNIT),
-        part(4, pk_hbm, pk, own0, nown),
-        part(5, pv_hbm, pv, own0, nown),
-        pltpu.make_async_copy(q_hbm, q, in_sem.at[6]),
-        pltpu.make_async_copy(k_hbm, k, in_sem.at[7]),
-        pltpu.make_async_copy(v_hbm, v, in_sem.at[8]),
-        pltpu.make_async_copy(dy_hbm, dy, in_sem.at[9]),
-        pltpu.make_async_copy(gain_hbm, gain_ref, in_sem.at[10]),
+        part(2, pk_hbm, pk, own0, UNIT),
+        part(3, pv_hbm, pv, own0, UNIT),
+        part(4, pk_hbm, pk, oth0 + UNIT, nown - UNIT),
+        part(5, pv_hbm, pv, oth0 + UNIT, nown - UNIT),
+        part(6, pk_hbm, pk, own0 + UNIT, nown - UNIT),
+        part(7, pv_hbm, pv, own0 + UNIT, nown - UNIT),
+        pltpu.make_async_copy(q_hbm, q, in_sem.at[8]),
+        pltpu.make_async_copy(k_hbm, k, in_sem.at[9]),
+        pltpu.make_async_copy(v_hbm, v, in_sem.at[10]),
+        pltpu.make_async_copy(dy_hbm, dy, in_sem.at[11]),
+        pltpu.make_async_copy(gain_hbm, gain_ref, in_sem.at[12]),
     ]
-    for c in loads[:6]:
+    for c in loads[:8]:
         c.start()
 
     barrier = pltpu.get_barrier_semaphore()
@@ -117,7 +145,7 @@
     inn[...] = jnp.zeros_like(inn)
     for c in loads[:2]:
         c.wait()
-    for c in loads[6:]:
+    for c in loads[8:]:
         c.start()
 
     def causal():
@@ -133,7 +161,7 @@
 
     plans = [timetable(nz, units, ph) for ph in range(2)]
 
-    def exchange(ph, produce, compute, consume, ready):
+    def exchange(ph, produce, compute, consume, ready, more):
         xo, xi, x, rin, rout, lin, lout, tot, tin = bufs[ph]
         pieces = units * SUB
 
@@ -168,27 +196,23 @@
             make(xo, u, oth0)
             to_partner(u).start()
 
-        def states(ref, u):
+        def state_of(ref, i):
             per = SUB // UNIT
-            return [
-                ref[u, j * per : (j + 1) * per].reshape(HEAD_DIM, HEAD_DIM) for j in range(UNIT)
-            ]
+            first = i % UNIT * per
+            return ref[i // UNIT, pl.ds(first, per)].reshape(HEAD_DIM, HEAD_DIM)
 
         make(xo, 0, oth0)
         ready(-2)
         to_partner(0).start()
         ready(-1)
-        plan = [pick([p[j] for p in plans[ph]]) for j in range(6)]
-        r_at, l_at, t_at, o_at, c_at, slots = plan
+        plan = [pick([p[j] for p in plans[ph]]) for j in range(12)]
+        r_at, l_at, t_at, o_at, slots = plan[:5]
+        total = 2 * units * STAGES
 
         def slot(s, carry):
             u = s // SUB
             fresh = s % SUB == 0
 
-            @pl.when(fresh & (u + 1 < units))
-            def _():
-                give(u + 1)
-
             @pl.when(fresh & (u < units))
             def _():
                 make(x, u, own0)
@@ -233,6 +257,17 @@
                 def _():
                     to_left(i_l).start()
 
+            more(s)
+
+            @pl.when(s == 0)
+            def _():
+                for ahead in range(1, min(AHEAD, units)):
+                    give(ahead)
+
+            @pl.when(fresh & (u + AHEAD < units))
+            def _():
+                give(u + AHEAD)
+
             i_t = s - t_at
 
             @pl.when((i_t >= 0) & (i_t < pieces))
@@ -249,31 +284,32 @@
 
                 total_out(i_t).start()
 
-            work = s - c_at
-            ready(work)
-
-            @pl.when((work >= 0) & (work < 2 * units * STAGES))
-            def _():
-                h = (own0 + work // STAGES * UNIT) % heads
+            def chunk(w, carry):
+                ready(w)
+                h = (own0 + w // STAGES * UNIT) % heads
                 for c in range(STAGES):
 
-                    @pl.when(work % STAGES == c)
+                    @pl.when(w % STAGES == c)
                     def _(c=c):
                         compute[c](h)
 
-            @pl.when((i_t >= 0) & (i_t < pieces) & (i_t % SUB == SUB - 1))
-            def _():
-                i = i_t // SUB
-                consume(own0 + i * UNIT, states(tot, i))
+                return carry
+
+            lax.fori_loop(done_by(s - 1, plan[5:], total), done_by(s, plan[5:], total), chunk, 0)
+
+            per = SUB // UNIT
+
+            @pl.when((i_t >= 0) & (i_t < pieces) & (i_t % per == per - 1))
+            def _():
+                consume(own0 + i_t // per, state_of(tot, i_t // per))
 
             i_o = s - o_at
 
-            @pl.when((i_o >= 0) & (i_o < pieces) & (i_o % SUB == SUB - 1))
-            def _():
-                i = i_o // SUB
-                for j in range(SUB):
-                    total_out(i * SUB + j).wait_recv()
-                consume(oth0 + i * UNIT, states(tin, i))
+            @pl.when((i_o >= 0) & (i_o < pieces) & (i_o % per == per - 1))
+            def _():
+                for j in range(per):
+                    total_out(i_o // per * per + j).wait_recv()
+                consume(oth0 + i_o // per, state_of(tin, i_o // per))
 
             return carry
 
@@ -319,35 +355,38 @@
                     barrier, nh + not_first.astype(jnp.int32) + not_last.astype(jnp.int32)
                 )
             else:
-                for c in loads[2:6]:
+                for c in loads[2:4]:
                     c.wait()
             return
 
         @pl.when(s == 0)
         def _():
-            for c in loads[6:9]:
+            for c in loads[8:11]:
                 c.wait()
 
         @pl.when(s == 1)
         def _():
-            loads[9].wait()
-            loads[10].wait()
-
-    def use_state(h, got):
+            loads[11].wait()
+            loads[12].wait()
+
+    def loaded_rest(s):
+        @pl.when(s == 0)
+        def _():
+            for c in loads[4:8]:
+                c.wait()
+
+    def use_state(h, state):
+        g = gain_ref[:, cs(h)]
         for c in range(nb):
             r = pl.ds(c * BLOCK, BLOCK)
-            squares, inner = sq[r, :], inn[r, :]
-            for j, state in enumerate(got):
-                st = (state if c == 0 else state + kv[h + j, c - 1]).astype(BF16)
-                mb[h + j, c] = st
-                oc = o[r, cs(h + j)] + mm(blk(q, c, h + j), st, 1, 0)
-                o[r, cs(h + j)] = oc
-                squares = squares + oc * oc
-                inner = inner + blk(dy, c, h + j).astype(F32) * gain_ref[:, cs(h + j)] * oc
-            sq[r, :] = squares
-            inn[r, :] = inner
-
-    exchange(0, prefix_part, (score, attend), use_state, loaded)
+            st = (state if c == 0 else state + kv[h, c - 1]).astype(BF16)
+            mb[h, c] = st
+            oc = o[r, cs(h)] + mm(blk(q, c, h), st, 1, 0)
+            o[r, cs(h)] = oc
+            sq[r, :] += oc * oc
+            inn[r, :] += blk(dy, c, h).astype(F32) * g * oc
+
+    exchange(0, prefix_part, (score, attend), use_state, loaded, loaded_rest)
 
     row_sq = jnp.sum(sq[...].T, axis=0, keepdims=True)
     row_in = jnp.sum(inn[...].T, axis=0, keepdims=True)
@@ -423,11 +462,10 @@
             stage[2][r, cs(h + j)] = kg.astype(BF16)
             stage[3][r, cs(h + j)] = vg.astype(BF16)
 
-    def keep_total(h, got):
-        for j, state in enumerate(got):
-            tout[h + j] = state
-
-    exchange(1, state_grad, (query_side, key_side), keep_total, lambda s: None)
+    def keep_total(h, state):
+        tout[h] = state
+
+    exchange(1, state_grad, (query_side, key_side), keep_total, lambda s: None, lambda s: None)
     for c in copies:
         c.wait_send()
 
@@ -441,21 +479,24 @@
     for j in range(4):
         pltpu.make_async_copy(ready[j], outs[j], sem.at[j]).start()
 
-    def head(h, carry):
-        c = pl.ds(pl.multiple_of(h * HEAD_DIM, HEAD_DIM), HEAD_DIM)
-        state = total[h]
-        hi = state.astype(BF16)
-        lo = (state - hi.astype(F32)).astype(BF16)
-        vals, keys = pv[:, c], pk[:, c]
-        vv = jnp.concatenate([vals, vals], axis=1)
-        kk = jnp.concatenate([keys, keys], axis=1)
-        pkg[:, c] = mm(vv, jnp.concatenate([hi, lo], axis=1), 1, 1).astype(BF16)
-        pvg[:, c] = mm(kk, jnp.concatenate([hi, lo], axis=0), 1, 0).astype(BF16)
+    def some(i, carry):
+        for j in range(GROUP):
+            h = i * GROUP + j
+            c = pl.ds(pl.multiple_of(h * HEAD_DIM, HEAD_DIM), HEAD_DIM)
+            state = total[h]
+            hi = state.astype(BF16)
+            lo = (state - hi.astype(F32)).astype(BF16)
+            vals, keys = pv[:, c], pk[:, c]
+            vv = jnp.concatenate([vals, vals], axis=1)
+            kk = jnp.concatenate([keys, keys], axis=1)
+            pkg[:, c] = mm(vv, jnp.concatenate([hi, lo], axis=1), 1, 1).astype(BF16)
+            pvg[:, c] = mm(kk, jnp.concatenate([hi, lo], axis=0), 1, 0).astype(BF16)
+        c = pl.ds(pl.multiple_of(i * GROUP * HEAD_DIM, HEAD_DIM), GROUP * HEAD_DIM)
         pltpu.make_async_copy(pkg.at[:, c], outs[4].at[:, c], sem.at[4]).start()
         pltpu.make_async_copy(pvg.at[:, c], outs[5].at[:, c], sem.at[5]).start()
         return carry
 
-    lax.fori_loop(0, heads, head, 0)
+    lax.fori_loop(0, heads // GROUP, some, 0)
     for j in range(4):
         pltpu.make_async_copy(ready[j], outs[j], sem.at[j]).wait()
     pltpu.make_async_copy(pkg, outs[4], sem.at[4]).wait()
@@ -493,7 +534,7 @@
         + states
         + states
         + [
-            pltpu.SemaphoreType.DMA((11,)),
+            pltpu.SemaphoreType.DMA((13,)),
             pltpu.SemaphoreType.DMA((max(nh - 1, 1),)),
             pltpu.SemaphoreType.DMA((max(nh - 1, 1),)),
             pltpu.SemaphoreType.DMA((2, 4)),

time: 64 us -> 61.3 us (0.958)
  Pallas kernels: 62.6 us -> 59.9 us
    pallas_call x1, Pallas kernels: 57 us -> 55.3 us  [body(): pl.pallas_call(functools.partial(kernel, nh, ns, float(cols * nh)), out_s...]
    pallas_call x1, Pallas kernels: 5.62 us -> 4.59 us  [body(): pl.pallas_call(finish, out_shape=[out] * 6, in_specs=[fast] * 7, out_spec...]
where the time goes in v2:
time: 61.3 us; the launch traced here: 61.1 us
  Pallas kernels  59.9 us (98%)
  between operations  1.29 us (2%)
    pallas_call x1, Pallas kernels, body(): pl.pallas_call(functools.partial(kernel, nh, ns, float(cols * nh)), out_s...  55.3 us
    pallas_call x1, Pallas kernels, body(): pl.pallas_call(finish, out_shape=[out] * 6, in_specs=[fast] * 7, out_spec...  4.59 us

profile of v2, /device:TPU:0, one launch (start us, length us, event | category | flops | bytes accessed | tf_op | source)
XLA Modules:
  0.0 61.1 jit_solution(4621830158197427221)
XLA Ops:
  1.3 55.3 %shard_map.127 = (bf16[512,2048]{1,0:T(8,128)(2,1)S(1)}, bf16[512,2048]{1,0:T(8,128)(2,1)S(1)}, bf16[512,2048]{1,0:T(8,128)(2,1)S(1)}, bf16[512,2048]{1,0:T(8,12...) custom-call(bf16[512,2048]{1,0:T(8,128)(2,1)} %refs_0_.1, ...), custom_call_target="tpu_custom_call" | custom-call | tf_op jit(solution)/shard_map/pallas_call | solution.py:550
  56.6 4.6 %shard_map.128 = (bf16[512,2048]{1,0:T(8,128)(2,1)}, bf16[512,2048]{1,0:T(8,128)(2,1)}, bf16[512,2048]{1,0:T(8,128)(2,1)}, bf16[512,2048]{1,0:T(8,128)(2,1)}, bf...) custom-call(bf16[512,2048]{1,0:T(8,128)(2,1)S(1)} %get-tuple-element.13.refs_0_, ...), custom_call_target="tpu_custom_call" | custom-call | tf_op jit(solution)/shard_map/pallas_call | solution.py:563

commit v3 on v2

--- a/solution.py
+++ b/solution.py
@@ -80,7 +80,7 @@
     (q, k, v, dy, do, o, sc, ps, kv, mb, gb, sq, inn, rinv, coef) = refs[15:30]
     st_out, st_in = refs[30:32]
     bufs = (refs[32:41], refs[41:50])
-    in_sem, st_send, st_recv, send_sem, recv_sem, gain_ref = refs[50:56]
+    in_sem, st_recv, given, recv_sem, gain_ref = refs[50:55]
 
     rows, cols = q.shape
     heads = cols // HEAD_DIM
@@ -169,8 +169,8 @@
             return pltpu.make_async_remote_copy(
                 src_ref=src,
                 dst_ref=dst,
-                send_sem=send_sem.at[ph, kind],
-                recv_sem=recv_sem.at[ph, kind, i],
+                send_sem=in_sem.at[kind],
+                recv_sem=given.at[ph, i] if kind == 0 else recv_sem.at[ph, kind - 1, i],
                 device_id=dev,
                 device_id_type=MESH,
             )
@@ -405,7 +405,7 @@
             pltpu.make_async_remote_copy(
                 src_ref=st_out,
                 dst_ref=st_in.at[d - 1],
-                send_sem=st_send.at[d - 1],
+                send_sem=in_sem.at[3 + d],
                 recv_sem=st_recv.at[d - 1],
                 device_id=((me_h + d) % nh, me_s),
                 device_id_type=MESH,
@@ -534,11 +534,10 @@
         + states
         + states
         + [
-            pltpu.SemaphoreType.DMA((13,)),
+            pltpu.SemaphoreType.DMA((max(13, 3 + nh),)),
             pltpu.SemaphoreType.DMA((max(nh - 1, 1),)),
-            pltpu.SemaphoreType.DMA((max(nh - 1, 1),)),
-            pltpu.SemaphoreType.DMA((2, 4)),
-            pltpu.SemaphoreType.DMA((2, 4, units * SUB)),
+            pltpu.SemaphoreType.DMA((2, units)),
+            pltpu.SemaphoreType.DMA((2, 3, units * SUB)),
             pltpu.VMEM((1, cols), F32),
         ]
     )

time: 61.3 us -> 61.1 us (level)
  no operation moved by 1% of the time
where the time goes in v3:
time: 61.1 us; the launch traced here: 61 us
  Pallas kernels  59.7 us (98%)
  between operations  1.29 us (2%)
    pallas_call x1, Pallas kernels, body(): pl.pallas_call(functools.partial(kernel, nh, ns, float(cols * nh)), out_s...  55.1 us
    pallas_call x1, Pallas kernels, body(): pl.pallas_call(finish, out_shape=[out] * 6, in_specs=[fast] * 7, out_spec...  4.59 us

profile of v3, /device:TPU:0, one launch (start us, length us, event | category | flops | bytes accessed | tf_op | source)
XLA Modules:
  0.0 61.0 jit_solution(15923587438868944031)
XLA Ops:
  1.3 55.1 %shard_map.127 = (bf16[512,2048]{1,0:T(8,128)(2,1)S(1)}, bf16[512,2048]{1,0:T(8,128)(2,1)S(1)}, bf16[512,2048]{1,0:T(8,128)(2,1)S(1)}, bf16[512,2048]{1,0:T(8,12...) custom-call(bf16[512,2048]{1,0:T(8,128)(2,1)} %refs_0_.1, ...), custom_call_target="tpu_custom_call" | custom-call | tf_op jit(solution)/shard_map/pallas_call | solution.py:549
  56.4 4.6 %shard_map.128 = (bf16[512,2048]{1,0:T(8,128)(2,1)}, bf16[512,2048]{1,0:T(8,128)(2,1)}, bf16[512,2048]{1,0:T(8,128)(2,1)}, bf16[512,2048]{1,0:T(8,128)(2,1)}, bf...) custom-call(bf16[512,2048]{1,0:T(8,128)(2,1)S(1)} %get-tuple-element.13.refs_0_, ...), custom_call_target="tpu_custom_call" | custom-call | tf_op jit(solution)/shard_map/pallas_call | solution.py:562

commit v4 on v3

--- a/solution.py
+++ b/solution.py
@@ -18,7 +18,7 @@
 SKEW = 3
 STAGES = 2
 AHEAD = 2
-GROUP = 4
+GROUP = 2
 PLAN = {
     4: (
         ([0, 3, 6, 9], [9, 6, 3, 0], [10, 7, 7, 10], [(4, 2, 1, 16, 99, 1, 1), (2, 1, 1, 16, 99, 1, 1), (2, 1, 1, 16, 99, 1, 1), (4, 2, 1, 16, 99, 1, 1)]),

time: 61.1 us -> 61.1 us (level)
  no operation moved by 1% of the time
where the time goes in v4:
time: 61.1 us; the launch traced here: 61 us
  Pallas kernels  59.7 us (98%)
  between operations  1.29 us (2%)
    pallas_call x1, Pallas kernels, body(): pl.pallas_call(functools.partial(kernel, nh, ns, float(cols * nh)), out_s...  55.1 us
    pallas_call x1, Pallas kernels, body(): pl.pallas_call(finish, out_shape=[out] * 6, in_specs=[fast] * 7, out_spec...  4.58 us

profile of v4, /device:TPU:0, one launch (start us, length us, event | category | flops | bytes accessed | tf_op | source)
XLA Modules:
  0.0 61.0 jit_solution(6472420665486333218)
XLA Ops:
  1.3 55.1 %shard_map.127 = (bf16[512,2048]{1,0:T(8,128)(2,1)S(1)}, bf16[512,2048]{1,0:T(8,128)(2,1)S(1)}, bf16[512,2048]{1,0:T(8,128)(2,1)S(1)}, bf16[512,2048]{1,0:T(8,12...) custom-call(bf16[512,2048]{1,0:T(8,128)(2,1)} %refs_0_.1, ...), custom_call_target="tpu_custom_call" | custom-call | tf_op jit(solution)/shard_map/pallas_call | solution.py:549
  56.4 4.6 %shard_map.128 = (bf16[512,2048]{1,0:T(8,128)(2,1)}, bf16[512,2048]{1,0:T(8,128)(2,1)}, bf16[512,2048]{1,0:T(8,128)(2,1)}, bf16[512,2048]{1,0:T(8,128)(2,1)}, bf...) custom-call(bf16[512,2048]{1,0:T(8,128)(2,1)S(1)} %get-tuple-element.13.refs_0_, ...), custom_call_target="tpu_custom_call" | custom-call | tf_op jit(solution)/shard_map/pallas_call | solution.py:562
